TPU v7x, 128 devices: a whole 4x4x4 slice. The times are simulated.
128 devices in a mesh: tm: 32 (over x, z, core), space: 4 (over y).
Axes of the slice: x: 4, y: 4, z: 4, core: 2. Of those that a mesh axis runs over, the one named last changes fastest.
Arguments:
- state: float32 [64, 3, 128, 1024], P('tm', None, 'space'), may hold values from -2.5 to 2.5
- initial: float32 [3, 128, 1024], P(None, 'space'), may hold values from -2.5 to 2.5
Outputs:
- updated: float32 [64, 3, 128, 1024], P('tm', None, 'space')
All inputs are finite; a program needn't handle non-finite values.
Results may differ from a plain program's by a relative error of at most 0.0003.
Values sent between devices are 32-bit elements; how exact they have to be, the bound alone decides.
A program may use at most 128 MiB of HBM per device.

v0:
```python
import math

import jax
import jax.numpy as jnp
from jax import lax
from jax.sharding import Mesh
from jax.sharding import PartitionSpec as P

SWEEPS = 4
TM = ("tm_0", "tm_1", "tm_2")


circulant_alpha = 0.1
time_step = 0.5
coriolis = 0.3
viscous = 0.2
highest = lax.Precision.HIGHEST


def from_behind(block, axis, distance):
    devices = range(lax.axis_size(axis))
    route = [(i - distance, i) for i in devices if i - distance in devices]
    return lax.ppermute(block, axis, route)


def extended(cells, sides, width):
    for axis, dim in sides:
        count = lax.axis_size(axis)
        head = lax.slice_in_dim(cells, 0, width, axis=dim)
        tail = lax.slice_in_dim(cells, cells.shape[dim] - width, cells.shape[dim], axis=dim)
        cells = jnp.concatenate(
            [
                lax.ppermute(tail, axis, [(i, (i + 1) % count) for i in range(count)]),
                cells,
                lax.ppermute(head, axis, [((i + 1) % count, i) for i in range(count)]),
            ],
            axis=dim,
        )
    return cells


def split_up(x, dim, length):
    before, after = (x.shape[:dim], x.shape[dim + 1 :])
    return jnp.moveaxis(x.reshape(*before, length, -1, *after), dim, 0)


def laid_out(pieces, dim):
    shape = list(pieces.shape[1:])
    shape[dim] *= pieces.shape[0]
    return jnp.moveaxis(pieces, 0, dim).reshape(shape)


def exchange_in_order(pieces, axes, sequence):
    inside = pieces.shape[1:]
    result = pieces.reshape(*(lax.axis_size(a) for a in axes), *inside)
    for k in sequence:
        result = lax.all_to_all(result, axes[k], k, k, tiled=True)
    return result.reshape(-1, *inside)


def two_step_exchange(x, groups, sequence, split_dim, concat_dim):
    length = lax.axis_size(groups[0]) * lax.axis_size(groups[1])
    pieces = split_up(x, split_dim, length)
    return laid_out(exchange_in_order(pieces, groups, sequence), concat_dim)


def interior(values):
    return values[..., 1:-1, :]


def trim_rows(values, width):
    return values[..., width : values.shape[-2] - width, :]


def column_diff(values):
    return 0.5 * (jnp.roll(values, -1, axis=-1) - jnp.roll(values, 1, axis=-1))[..., 1:-1, :]


def row_diff(values):
    return 0.5 * (values[..., 2:, :] - values[..., :-2, :])


def laplace(values):
    return (
        values[..., 2:, :]
        + values[..., :-2, :]
        + jnp.roll(values, -1, axis=-1)[..., 1:-1, :]
        + jnp.roll(values, 1, axis=-1)[..., 1:-1, :]
        - 4.0 * values[..., 1:-1, :]
    )


def tendency(padded):
    surface = padded[..., 0, :, :]
    eastward = padded[..., 1, :, :]
    northward = padded[..., 2, :, :]
    column_depth = 1.0 + surface
    east_inner = interior(eastward)
    north_inner = interior(northward)
    mass_change = time_step * (
        column_diff(column_depth * eastward) + row_diff(column_depth * northward)
    ) - viscous * laplace(surface)
    east_change = (
        time_step
        * (
            east_inner * column_diff(eastward)
            + north_inner * row_diff(eastward)
            + column_diff(surface)
        )
        - coriolis * north_inner
        - viscous * laplace(eastward)
    )
    north_change = (
        time_step
        * (
            east_inner * column_diff(northward)
            + north_inner * row_diff(northward)
            + row_diff(surface)
        )
        + coriolis * east_inner
        - viscous * laplace(northward)
    )
    return jnp.stack([mass_change, east_change, north_change], axis=-3)


def linear_part(padded):
    surface = padded[..., 0, :, :]
    eastward = padded[..., 1, :, :]
    northward = padded[..., 2, :, :]
    mass_change = time_step * (column_diff(eastward) + row_diff(northward)) - viscous * laplace(
        surface
    )
    east_change = (
        time_step * column_diff(surface)
        - coriolis * interior(northward)
        - viscous * laplace(eastward)
    )
    north_change = (
        time_step * row_diff(surface) + coriolis * interior(eastward) - viscous * laplace(northward)
    )
    return jnp.stack([mass_change, east_change, north_change], axis=-3)


def pair_apply(factors, values):
    factor = factors[:, :, None, None, None]
    return jnp.stack(
        [
            factor[0] * values[0] - factor[1] * values[1],
            factor[2] * values[1] + factor[3] * values[0],
        ]
    )


def sweep_weights():
    return [
        1.0 / (1.15 - 0.85 * math.cos(math.pi * (2 * sweep + 1) / (2 * SWEEPS)))
        for sweep in range(SWEEPS)
    ]


def slot_factors(slot_index, total_steps):
    decay_base = circulant_alpha ** (1.0 / total_steps)
    angles = 2.0 * math.pi / total_steps * slot_index.astype(jnp.float32)
    real_eigen = 1.0 - decay_base * jnp.cos(angles)
    imaginary_eigen = decay_base * jnp.sin(angles)
    real_shift = real_eigen + 4.0 * viscous
    modulus = real_shift * real_shift + imaginary_eigen * imaginary_eigen
    eigen = jnp.stack([real_eigen, imaginary_eigen, real_eigen, imaginary_eigen])
    jacobi = jnp.stack(
        [
            real_shift / modulus,
            -imaginary_eigen / modulus,
            real_shift / modulus,
            -imaginary_eigen / modulus,
        ]
    )
    leading = (slot_index == 0)[None, :]
    zero_part = jnp.zeros_like(real_eigen)
    packed_eigen = jnp.stack(
        [zero_part + (1.0 - decay_base), zero_part, zero_part + (1.0 + decay_base), zero_part]
    )
    packed_jacobi = jnp.stack(
        [
            zero_part + 1.0 / (1.0 - decay_base + 4.0 * viscous),
            zero_part,
            zero_part + 1.0 / (1.0 + decay_base + 4.0 * viscous),
            zero_part,
        ]
    )
    eigen = jnp.where(leading, packed_eigen, eigen)
    jacobi = jnp.where(leading, packed_jacobi, jacobi)
    return (eigen, jacobi)


def time_tables(total_steps):
    slot_total = total_steps // 2
    step_ids = jnp.arange(total_steps, dtype=jnp.int32)
    slot_ids = jnp.arange(slot_total, dtype=jnp.int32)
    phase = slot_ids[:, None] * step_ids[None, :] % total_steps
    angles = 2.0 * math.pi / total_steps * phase.astype(jnp.float32)
    decay_base = circulant_alpha ** (1.0 / total_steps)
    growth = decay_base ** step_ids.astype(jnp.float32)
    cosine = jnp.cos(angles)
    sines = jnp.sin(angles)
    forward_real = cosine * growth[None, :]
    forward_imaginary = -sines * growth[None, :]
    inverse_imaginary = -sines
    alternate = 1.0 - 2.0 * (step_ids % 2).astype(jnp.float32)
    leading = (slot_ids == 0)[:, None]
    forward_imaginary = jnp.where(leading, (alternate * growth)[None, :], forward_imaginary)
    inverse_real = jnp.where(leading, 1.0, 2.0 * cosine)
    inverse_imaginary = jnp.where(leading, alternate[None, :], -2.0 * sines)
    forward = jnp.concatenate([forward_real, forward_imaginary], axis=0)
    inverse = jnp.concatenate([inverse_real, inverse_imaginary], axis=0).T
    inverse = inverse * (1.0 / (total_steps * growth))[:, None]
    return (forward, inverse)


def on_device(state, initial):
    steps_dev, fields, band_rows, columns = state.shape
    width_tm = lax.axis_size(TM)
    total_steps = steps_dev * width_tm
    previous = from_behind(state[-1], TM, 1)
    previous = jnp.where(lax.axis_index(TM) == 0, initial, previous)
    before = jnp.concatenate([previous[None], state[:-1]], axis=0)
    padded = extended(state, (("space", 2),), 1)
    residual = state - before + tendency(padded)
    forward, inverse = time_tables(total_steps)
    slot_total = forward.shape[0] // 2
    per_device = slot_total // width_tm
    spectrum = jnp.einsum(
        "rj,jnc->rnc",
        forward,
        two_step_exchange(
            residual.reshape(steps_dev, fields, band_rows * columns),
            (("tm_0", "tm_1"), "tm_2"),
            (1, 0),
            2,
            0,
        ),
        precision=highest,
    )
    spectrum = spectrum.reshape(2, slot_total, fields, spectrum.shape[-1])
    banded = two_step_exchange(spectrum, (("tm_0", "tm_1"), "tm_2"), (0, 1), 1, 3).reshape(
        2, per_device, fields, band_rows, columns
    )
    slot_index = lax.axis_index(TM) * per_device + jnp.arange(per_device, dtype=jnp.int32)
    eigen, jacobi = slot_factors(slot_index, total_steps)
    weights = sweep_weights()
    widened = extended(banded, (("space", 3),), SWEEPS - 1)
    iterate = weights[0] * pair_apply(jacobi, widened)
    for sweep in range(1, SWEEPS):
        applied = pair_apply(eigen, interior(iterate)) + linear_part(iterate)
        iterate = interior(iterate) + weights[sweep] * pair_apply(
            jacobi, trim_rows(widened, sweep) - applied
        )
    flat_solution = iterate.reshape(2, per_device, fields, band_rows * columns)
    blocks = two_step_exchange(flat_solution, (("tm_0", "tm_1"), "tm_2"), (1, 0), 3, 1)
    merged = blocks.reshape(2 * blocks.shape[1], blocks.shape[2], blocks.shape[3])
    all_steps = jnp.einsum("jr,rnc->jnc", inverse, merged, precision=highest)
    correction = two_step_exchange(all_steps, (("tm_0", "tm_1"), "tm_2"), (1, 0), 0, 2)
    return state - correction.reshape(state.shape)


def solution(mesh):
    split = Mesh(
        mesh.devices.reshape(4, 4, 2, mesh.shape["space"]), ("tm_0", "tm_1", "tm_2", "space")
    )
    return jax.shard_map(
        on_device,
        mesh=split,
        in_specs=(P(TM, None, "space", None), P(None, "space", None)),
        out_specs=P(TM, None, "space", None),
        check_vma=False,
    )
```

profile of v0, /device:TPU:1, one launch (start us, length us, event | category | flops | bytes accessed | tf_op | source)
XLA Modules:
  0.0 178.7 jit_solution(5542156236541247116)
XLA Ops:
  0.0 1.1 fusion.136
  1.1 2.2 %collective-permute-start.1 = (f32[2,3,1,1024]{3,2,0,1:T(1,128)S(1)}, f32[2,3,1,1024]{3,2,0,1:T(1,128)S(1)}, u32[]{:S(2)}, u32[]{:S(2)}) collective-permute-start(f32[2,3,1,1024]{3,2,0,1:T(1,128)S(1)} %get-tuple-element.37), channel_id=1, source_target_pairs={{0,1},{1,2},{2,3},{3,0},{4,5},{5,6},{6,7},{7,4},{8,9},{9,10},{10,1... | collective-permute-start | bytes 73736 | tf_op jit(solution)/shard_map/ppermute | solution.py:33
  3.2 1.5 collective-permute-start.2
  4.8 1.2 slice_bitcast_fusion
  5.9 4.5 %collective-permute-start = (f32[3,32,1024]{2,1,0:T(8,128)S(1)}, f32[3,32,1024]{2,1,0:T(8,128)S(1)}, u32[]{:S(2)}, u32[]{:S(2)}) collective-permute-start(f32[3,32,1024]{2,1,0:T(8,128)S(1)} %get-tuple-element.39), channel_id=1, source_target_pairs={{0,4},{4,8},{8,12},{12,16},{16,20},{20,24},{24,28},{28,32},{32,36}... | collective-permute-start | bytes 1179656 | tf_op jit(solution)/shard_map/ppermute | solution.py:23
  12.8 2.4 %collective-permute-done = f32[3,32,1024]{2,1,0:T(8,128)S(1)} collective-permute-done((f32[3,32,1024]{2,1,0:T(8,128)S(1)}, f32[3,32,1024]{2,1,0:T(8,128)S(1)}, u32[]{:S(2)}, u32[]{:S(2)}) %collective-permute-start) | collective-permute-done | bytes 393248 | tf_op jit(solution)/shard_map/ppermute | solution.py:23
  16.1 4.0 %all_to_all.40 = f32[16,2,2,3,1024]{4,2,0,3,1:T(2,128)S(1)} all-to-all(f32[16,2,2,3,1024]{4,2,0,3,1:T(2,128)S(1)} %copy.148), channel_id=1, replica_groups=mesh['tm_0'=4,'tm_1'=4,'tm_2'=2,'space'=4] {'tm_2'}, dimensions={1} | all-to-all | bytes 1572864 | tf_op jit(solution)/shard_map/all_to_all | solution.py:57
  20.1 1.0 copy.149
  21.1 8.5 %all-to-all-start.1 = ((f32[16,2,2,3,1024]{4,2,1,3,0:T(2,128)}), f32[16,2,2,3,1024]{4,2,1,3,0:T(2,128)S(1)}, u32[]{:S(2)}, u32[]{:S(2)}) async-start(f32[16,2,2,3,1024]{4,2,1,3,0:T(2,128)} %copy.149), calls=%async_computation.1 | async-start | bytes 1572864 | tf_op jit(solution)/shard_map/all_to_all | solution.py:57
  30.1 12.4 %all-to-all-done.1 = f32[16,2,2,3,1024]{4,2,1,3,0:T(2,128)S(1)} async-done(((f32[16,2,2,3,1024]{4,2,1,3,0:T(2,128)}), f32[16,2,2,3,1024]{4,2,1,3,0:T(2,128)S(1)}, u32[]{:S(2)}, u32[]{:S(2)}) %all-to-all-start.1) | async-done | bytes 786464 | tf_op jit(solution)/shard_map/all_to_all | solution.py:57
  43.0 0.8 convolution_bitcast_fusion
  44.3 1.0 copy.151
  45.3 4.3 %all-to-all-start.2 = ((f32[16,2,2,1,3,1024]{5,1,4,2,3,0:T(2,128)}), f32[16,2,2,1,3,1024]{5,1,4,2,3,0:T(2,128)S(1)}, u32[]{:S(2)}, u32[]{:S(2)}) async-start(f32[16,2,2,1,3,1024]{5,1,4,2,3,0:T(2,128)} %copy.151), calls=%async_computation.2 | async-start | bytes 1572864 | tf_op jit(solution)/shard_map/all_to_all | solution.py:57
  49.8 0.6 copy-done.2
  50.5 0.7 fusion.164
  51.2 10.4 %all-to-all-done.2 = f32[16,2,2,1,3,1024]{5,1,4,2,3,0:T(2,128)S(1)} async-done(((f32[16,2,2,1,3,1024]{5,1,4,2,3,0:T(2,128)}), f32[16,2,2,1,3,1024]{5,1,4,2,3,0:T(2,128)S(1)}, u32[]{:S(2)}, u32[]{:S(2)}) %all-to-all-start.2) | async-done | bytes 786464 | tf_op jit(solution)/shard_map/all_to_all | solution.py:57
  62.1 7.2 %all_to_all.41 = f32[16,2,2,1,3,1024]{5,0,4,2,3,1:T(8,128)S(1)} all-to-all(f32[16,2,2,1,3,1024]{5,0,4,2,3,1:T(8,128)S(1)} %copy.152), channel_id=1, replica_groups=mesh['tm_0'=4,'tm_1'=4,'tm_2'=2,'space'=4] {'tm_2'}, dimensions={1} | all-to-all | bytes 1572864 | tf_op jit(solution)/shard_map/all_to_all | solution.py:57
  70.1 0.7 fusion.163
  70.7 12.8 %collective-permute-start.4 = (f32[2,1,3,3,1024]{4,0,3,2,1:T(2,128)S(1)}, f32[2,1,3,3,1024]{4,0,3,2,1:T(2,128)S(1)}, u32[]{:S(2)}, u32[]{:S(2)}) collective-permute-start(f32[2,1,3,3,1024]{4,0,3,2,1:T(2,128)S(1)} %copy.196), channel_id=1, source_target_pairs={{1,0},{2,1},{3,2},{0,3},{5,4},{6,5},{7,6},{4,7},{9,8},{10,9},{11,1... | collective-permute-start | bytes 221192 | tf_op jit(solution)/shard_map/ppermute | solution.py:35
  83.7 1.3 collective-permute-done.4
  85.0 3.4 %multiply_subtract_fusion = (f32[1,1,3,38,1024]{4,0,3,2,1:T(1,128)S(1)}, f32[1,1,3,38,1024]{4,0,3,2,1:T(1,128)S(1)}) fusion(f32[2,1,3,38,1024]{4,0,3,2,1:T(2,128)S(1)} %constant_dynamic-update-slice_fusion, f32[]{:T(128)} %bitcast.31, f32[]{:T(128)} %bitcast.8, f32[]{:T(128)} %bitcast.33, f32[]{:T(128)} %bitcast.32), kind=kLoop, calls=%fused_computation.22 | loop fusion | flops 700416 | bytes 1867792 | tf_op jit(solution)/shard_map/sub | solution.py:148
  88.4 1.0 maximum_multiply_fusion
  90.5 1.3 subtract_bitcast_fusion
  91.8 0.9 fusion.28
  93.2 0.7 fusion.27
  93.9 3.5 %multiply_subtract_fusion.2 = (f32[1,1,3,36,1024]{4,0,3,2,1:T(1,128)S(1)}, f32[1,1,3,36,1024]{4,0,3,2,1:T(1,128)S(1)}) fusion(f32[2,1,3,38,1024]{4,0,3,2,1:T(2,128)S(1)} %maximum_multiply_fusion, f32[]{:T(128)} %bitcast.37, f32[]{:T(128)} %bitcast.36, f32[]{:T(128)} %bitcast.39, f32[]{:T(128)} %bitcast.38), kind=kLoop, calls=%fused_computation.26 | loop fusion | flops 663552 | bytes 1769488 | tf_op jit(solution)/shard_map/sub | solution.py:148
  97.4 1.3 slice_subtract_fusion
  98.7 3.4 %multiply_subtract_fusion.1 = (f32[1,1,3,36,1024]{4,0,3,2,1:T(1,128)S(1)}, f32[1,1,3,36,1024]{4,0,3,2,1:T(1,128)S(1)}) fusion(f32[2,1,3,36,1024]{4,0,3,2,1:T(2,128)S(1)} %slice_subtract_fusion, f32[]{:T(128)} %bitcast.31, f32[]{:T(128)} %bitcast.8, f32[]{:T(128)} %bitcast.33, f32[]{:T(128)} %bitcast.32), kind=kLoop, calls=%fused_computation.24 | loop fusion | flops 663552 | bytes 1769488 | tf_op jit(solution)/shard_map/sub | solution.py:148
  102.1 1.1 slice_add_fusion
  104.2 1.2 subtract_bitcast_fusion.1
  105.5 0.9 fusion.52
  106.9 3.5 %multiply_subtract_fusion.4 = (f32[1,1,3,34,1024]{4,0,3,2,1:T(1,128)S(1)}, f32[1,1,3,34,1024]{4,0,3,2,1:T(1,128)S(1)}) fusion(f32[2,1,3,36,1024]{4,0,3,2,1:T(2,128)S(1)} %slice_add_fusion, f32[]{:T(128)} %bitcast.37, f32[]{:T(128)} %bitcast.36, f32[]{:T(128)} %bitcast.39, f32[]{:T(128)} %bitcast.38), kind=kLoop, calls=%fused_computation.30 | loop fusion | flops 626688 | bytes 1671184 | tf_op jit(solution)/shard_map/sub | solution.py:148
  110.3 0.6 fusion.51
  111.0 1.3 fusion
  112.3 3.3 %multiply_subtract_fusion.3 = (f32[1,1,3,34,1024]{4,0,2,3,1:T(1,128)S(1)}, f32[1,1,3,34,1024]{4,0,2,3,1:T(1,128)S(1)}) fusion(f32[2,1,3,34,1024]{4,0,2,3,1:T(2,128)S(1)} %fusion, f32[]{:T(128)} %bitcast.31, f32[]{:T(128)} %bitcast.8, f32[]{:T(128)} %bitcast.33, f32[]{:T(128)} %bitcast.32), kind=kLoop, calls=%fused_computation.28 | loop fusion | flops 626688 | bytes 1671184 | tf_op jit(solution)/shard_map/sub | solution.py:148
  115.7 1.0 fusion.1
  117.7 0.8 subtract_bitcast_fusion.2
  118.5 0.8 fusion.119
  120.4 3.2 %multiply_subtract_fusion.6 = (f32[1,1,3,32,1024]{4,0,3,2,1:T(1,128)S(1)}, f32[1,1,3,32,1024]{4,0,3,2,1:T(1,128)S(1)}) fusion(f32[1,1,3,32,1024]{4,0,2,3,1:T(1,128)S(1)} %get-tuple-element.28, f32[1,1,3,32,1024]{4,0,2,3,1:T(1,128)S(1)} %get-tuple-element.27, f32[]{:T(128)} %bitcast.37, f32[]{:T(128)} %bitcast.36, f32[]{:T(128)} %bitcast.39, f32[]{:T(128)} %bitcast.38), kind=kLoop, calls=%fused_computation.34 | loop fusion | flops 589824 | bytes 1572880 | tf_op jit(solution)/shard_map/sub | solution.py:148
  124.3 1.0 copy_subtract_fusion
  125.3 3.3 %multiply_subtract_fusion.5 = (f32[1,1,3,32,1024]{4,0,2,3,1:T(1,128)S(1)}, f32[1,1,3,32,1024]{4,0,2,3,1:T(1,128)S(1)}) fusion(f32[2,1,3,32,1024]{4,0,2,3,1:T(2,128)S(1)} %copy_subtract_fusion, f32[]{:T(128)} %bitcast.31, f32[]{:T(128)} %bitcast.8, f32[]{:T(128)} %bitcast.33, f32[]{:T(128)} %bitcast.32), kind=kLoop, calls=%fused_computation.32 | loop fusion | flops 589824 | bytes 1572880 | tf_op jit(solution)/shard_map/sub | solution.py:148
  128.6 1.0 slice_add_fusion.1
  130.1 5.5 %all_to_all.42 = f32[16,2,2,1,3,1024]{5,0,2,4,3,1:T(8,128)S(1)} all-to-all(f32[16,2,2,1,3,1024]{5,0,2,4,3,1:T(8,128)S(1)} %copy.167), channel_id=1, replica_groups=mesh['tm_0'=4,'tm_1'=4,'tm_2'=2,'space'=4] {'tm_2'}, dimensions={1} | all-to-all | bytes 1572864 | tf_op jit(solution)/shard_map/all_to_all | solution.py:57
  136.2 16.7 %all_to_all.43 = f32[16,2,2,1,3,1024]{5,1,2,4,3,0:T(2,128)S(1)} all-to-all(f32[16,2,2,1,3,1024]{5,1,2,4,3,0:T(2,128)S(1)} %copy.168), channel_id=1, replica_groups=mesh['tm_0'=4,'tm_1'=4,'tm_2'=2,'space'=4] {'tm_0','tm_1'}, dimensions={0} | all-to-all | bytes 1572864 | tf_op jit(solution)/shard_map/all_to_all | solution.py:57
  153.5 0.8 fusion.123
  154.3 5.8 %all_to_all.44 = f32[16,2,2,3,1024]{4,0,3,2,1:T(8,128)S(1)} all-to-all(f32[16,2,2,3,1024]{4,0,3,2,1:T(8,128)S(1)} %fusion.123), channel_id=1, replica_groups=mesh['tm_0'=4,'tm_1'=4,'tm_2'=2,'space'=4] {'tm_2'}, dimensions={1} | all-to-all | bytes 1572864 | tf_op jit(solution)/shard_map/all_to_all | solution.py:57
  160.6 16.5 %all_to_all.45 = f32[16,2,2,3,1024]{4,2,3,1,0:T(2,128)S(1)} all-to-all(f32[16,2,2,3,1024]{4,2,3,1,0:T(2,128)S(1)} %copy.172), channel_id=1, replica_groups=mesh['tm_0'=4,'tm_1'=4,'tm_2'=2,'space'=4] {'tm_0','tm_1'}, dimensions={0} | all-to-all | bytes 1572864 | tf_op jit(solution)/shard_map/all_to_all | solution.py:57
  177.1 1.2 bitcast_subtract_fusion
  (75 shorter events, 14.0 us)
Async XLA Ops:
  1.1 9.4 %collective-permute-start.1 = (f32[2,3,1,1024]{3,2,0,1:T(1,128)S(1)}, f32[2,3,1,1024]{3,2,0,1:T(1,128)S(1)}, u32[]{:S(2)}, u32[]{:S(2)}) collective-permute-start(f32[2,3,1,1024]{3,2,0,1:T(1,128)S(1)} %get-tuple-element.37), channel_id=1, source_target_pairs={{0,1},{1,2},{2,3},{3,0},{4,5},{5,6},{6,7},{7,4},{8,9},{9,10},{10,1... | collective-permute-start | bytes 73736 | tf_op jit(solution)/shard_map/ppermute | solution.py:33
  3.2 7.3 %copy-start = (f32[2,3,32,1024]{3,2,1,0:T(8,128)S(1)}, f32[2,3,32,1024]{3,2,1,0:T(8,128)}, u32[]{:S(2)}) copy-start(f32[2,3,32,1024]{3,2,1,0:T(8,128)} %param.2) | copy-start | bytes 2359300
  3.2 7.3 %collective-permute-start.2 = (f32[2,3,1,1024]{3,2,0,1:T(1,128)S(1)}, f32[2,3,1,1024]{3,2,0,1:T(1,128)S(1)}, u32[]{:S(2)}, u32[]{:S(2)}) collective-permute-start(f32[2,3,1,1024]{3,2,0,1:T(1,128)S(1)} %get-tuple-element.38), channel_id=1, source_target_pairs={{1,0},{2,1},{3,2},{0,3},{5,4},{6,5},{7,6},{4,7},{9,8},{10,9},{11,1... | collective-permute-start | bytes 73736 | tf_op jit(solution)/shard_map/ppermute | solution.py:35
  5.9 9.2 %collective-permute-start = (f32[3,32,1024]{2,1,0:T(8,128)S(1)}, f32[3,32,1024]{2,1,0:T(8,128)S(1)}, u32[]{:S(2)}, u32[]{:S(2)}) collective-permute-start(f32[3,32,1024]{2,1,0:T(8,128)S(1)} %get-tuple-element.39), channel_id=1, source_target_pairs={{0,4},{4,8},{8,12},{12,16},{16,20},{20,24},{24,28},{28,32},{32,36}... | collective-permute-start | bytes 1179656 | tf_op jit(solution)/shard_map/ppermute | solution.py:23
  12.4 2.7 %copy-start.1 = (f32[3,32,1024]{2,1,0:T(8,128)S(1)}, f32[3,32,1024]{2,1,0:T(8,128)}, u32[]{:S(2)}) copy-start(f32[3,32,1024]{2,1,0:T(8,128)} %param.3) | copy-start | bytes 1179652
  21.1 21.3 %all-to-all-start.1 = ((f32[16,2,2,3,1024]{4,2,1,3,0:T(2,128)}), f32[16,2,2,3,1024]{4,2,1,3,0:T(2,128)S(1)}, u32[]{:S(2)}, u32[]{:S(2)}) async-start(f32[16,2,2,3,1024]{4,2,1,3,0:T(2,128)} %copy.149), calls=%async_computation.1 | async-start | bytes 1572864 | tf_op jit(solution)/shard_map/all_to_all | solution.py:57
  45.3 16.3 %all-to-all-start.2 = ((f32[16,2,2,1,3,1024]{5,1,4,2,3,0:T(2,128)}), f32[16,2,2,1,3,1024]{5,1,4,2,3,0:T(2,128)S(1)}, u32[]{:S(2)}, u32[]{:S(2)}) async-start(f32[16,2,2,1,3,1024]{5,1,4,2,3,0:T(2,128)} %copy.151), calls=%async_computation.2 | async-start | bytes 1572864 | tf_op jit(solution)/shard_map/all_to_all | solution.py:57
  49.8 0.7 copy-start.2
  49.8 0.7 copy-start.3
  69.9 13.7 %collective-permute-start.3 = (f32[2,1,3,3,1024]{4,0,3,2,1:T(2,128)S(1)}, f32[2,1,3,3,1024]{4,0,3,2,1:T(2,128)S(1)}, u32[]{:S(2)}, u32[]{:S(2)}) collective-permute-start(f32[2,1,3,3,1024]{4,0,3,2,1:T(2,128)S(1)} %copy.195), channel_id=1, source_target_pairs={{0,1},{1,2},{2,3},{3,0},{4,5},{5,6},{6,7},{7,4},{8,9},{9,10},{10,1... | collective-permute-start | bytes 221192 | tf_op jit(solution)/shard_map/ppermute | solution.py:33
  70.7 14.2 %collective-permute-start.4 = (f32[2,1,3,3,1024]{4,0,3,2,1:T(2,128)S(1)}, f32[2,1,3,3,1024]{4,0,3,2,1:T(2,128)S(1)}, u32[]{:S(2)}, u32[]{:S(2)}) collective-permute-start(f32[2,1,3,3,1024]{4,0,3,2,1:T(2,128)S(1)} %copy.196), channel_id=1, source_target_pairs={{1,0},{2,1},{3,2},{0,3},{5,4},{6,5},{7,6},{4,7},{9,8},{10,9},{11,1... | collective-permute-start | bytes 221192 | tf_op jit(solution)/shard_map/ppermute | solution.py:35
where the time goes:
time: 182 us; the launch traced here: 179 us
  blocking collectives  55.6 us (31%)
  other arithmetic  42.5 us (23%)
  starting transfers between devices  34 us (19%)
  waiting for transfers between devices  26.4 us (15%)
  local copies, waits for them, and re-layouts  17.4 us (10%)
    all_to_all x6, blocking collectives, exchange_in_order(): result = lax.all_to_all(result, axes[k], k, k, tiled=True)  55.6 us
    sub x7, other arithmetic, pair_apply(): factor[0] * values[0] - factor[1] * values[1]  23.6 us
    all_to_all x2, waiting for transfers between devices, exchange_in_order(): result = lax.all_to_all(result, axes[k], k, k, tiled=True)  22.8 us
    ppermute x2, starting transfers between devices, extended(): lax.ppermute(head, axis, [((i + 1) % count, i) for i in range(count)])  14.3 us
    all_to_all x2, starting transfers between devices, exchange_in_order(): result = lax.all_to_all(result, axes[k], k, k, tiled=True)  12.8 us
    another operation x9, other arithmetic, linear_part(): return jnp.stack([mass_change, east_change, north_change], axis=-3)  7.94 us
    ppermute x1, starting transfers between devices, from_behind(): return lax.ppermute(block, axis, route)  4.52 us
    all_to_all x7, local copies, waits for them, and re-layouts, exchange_in_order(): result = lax.all_to_all(result, axes[k], k, k, tiled=True)  3.73 us
  transfers between devices with their start and end apart: 7, of which 4 were waited for; matrix products, arithmetic and copies ran while one was open for 3% of the time, Pallas kernels for 0%

commit v1 on v0

v1 whole, which is shorter than its diff:
```python
import functools
import math

import jax
import jax.numpy as jnp
from jax import lax
from jax.experimental import pallas as pl
from jax.experimental.pallas import tpu as pltpu
from jax.sharding import PartitionSpec as P

SWEEPS = 4
ALPHA = 0.1
A = 1.0 / 1.8
R = 40
MESH = pl.DeviceIdType.MESH
f32 = jnp.float32


def sweep_weights():
    return [
        1.0 / (1.15 - 0.85 * math.cos(math.pi * (2 * m + 1) / (2 * SWEEPS))) for m in range(SWEEPS)
    ]


def residual_tile(load, j, before):
    sub = lax.broadcasted_iota(jnp.int32, (8, 1), 0)

    def near(f):
        here, after, ahead = load(f, j), load(f, (j + 1) % 5), load(f, (j + 4) % 5)
        cols = here.shape[1]
        north = pltpu.roll(jnp.where(sub == 0, after, here), 7, 0)
        south = pltpu.roll(jnp.where(sub == 7, ahead, here), 1, 0)
        east = pltpu.roll(here, cols - 1, 1)
        west = pltpu.roll(here, 1, 1)
        return here, east, west, north, south

    e, ee, ew, en, es = near(0)
    u, ue, uw, un, us = near(1)
    v, ve, vw, vn, vs = near(2)
    mass = 0.25 * (
        ((1.0 + ee) * ue - (1.0 + ew) * uw) + ((1.0 + en) * vn - (1.0 + es) * vs)
    ) - 0.2 * (ee + ew + en + es - 4.0 * e)
    east = (
        0.25 * (u * (ue - uw) + v * (un - us) + (ee - ew))
        - 0.3 * v
        - 0.2 * (ue + uw + un + us - 4.0 * u)
    )
    north = (
        0.25 * (u * (ve - vw) + v * (vn - vs) + (en - es))
        + 0.3 * u
        - 0.2 * (ve + vw + vn + vs - 4.0 * v)
    )
    return [x - before(f, j) + t for f, (x, t) in enumerate(((e, mass), (u, east), (v, north)))]


def kernel(
    ntm,
    nsp,
    state,
    initial,
    out,
    halo,
    prev,
    prev_halo,
    res,
    send,
    s_buf,
    y_buf,
    corr,
    back,
    ex_send,
    ex_recv,
    in_send,
    in_recv,
    back_send,
    back_recv,
):
    me = lax.axis_index("tm")
    sp = lax.axis_index("space")
    nxt, prv = lax.rem(me + 1, ntm), lax.rem(me + ntm - 1, ntm)
    up, dn = lax.rem(sp + 1, nsp), lax.rem(sp + nsp - 1, nsp)
    cols = state.shape[3]
    steps = 2 * ntm
    width = cols // ntm
    sub8 = lax.broadcasted_iota(jnp.int32, (8, 1), 0)

    barrier = pltpu.get_barrier_semaphore()
    around = [(me, up), (me, dn), (nxt, up), (nxt, dn), (prv, up), (prv, dn)]
    for other in around:
        pl.semaphore_signal(barrier, inc=1, device_id=other, device_id_type=MESH)

    def greet(k, carry):
        pl.semaphore_signal(
            barrier, inc=1, device_id=(lax.rem(me + k, ntm), sp), device_id_type=MESH
        )
        return carry

    lax.fori_loop(1, ntm, greet, 0)
    pl.semaphore_wait(barrier, ntm - 1 + len(around))

    def exchange(i, src, dst, device):
        return pltpu.make_async_remote_copy(
            src_ref=src,
            dst_ref=dst,
            send_sem=ex_send.at[i],
            recv_sem=ex_recv.at[i],
            device_id=device,
            device_id_type=MESH,
        )

    low, high = pl.ds(0, 4), pl.ds(4, 4)
    rows_hi = pl.ds(28, 4)

    def edges():
        return [
            exchange(0, state.at[:, :, low], halo.at[:, :, low], (me, dn)),
            exchange(1, state.at[:, :, rows_hi], halo.at[:, :, high], (me, up)),
        ]

    def handed(last):
        return [
            exchange(2, last, prev, (nxt, sp)),
            exchange(3, last.at[:, low], prev_halo.at[:, low], (nxt, dn)),
            exchange(4, last.at[:, rows_hi], prev_halo.at[:, high], (nxt, up)),
        ]

    normal = edges() + handed(state.at[1])
    for copy in normal[:2]:
        copy.start()

    @pl.when(me != ntm - 1)
    def _():
        for copy in normal[2:]:
            copy.start()

    @pl.when(me == ntm - 1)
    def _():
        for copy in handed(initial):
            copy.start()

    def in_copy(t, p, slot):
        return pltpu.make_async_remote_copy(
            src_ref=send.at[t, p],
            dst_ref=s_buf.at[slot],
            send_sem=in_send.at[t, p],
            recv_sem=in_recv.at[t, lax.div(slot, 2)],
            device_id=(p, sp),
            device_id_type=MESH,
        )

    res[3 * R :, :] = jnp.zeros((res.shape[0] - 3 * R, cols), f32)

    def step_out(t):
        def load(f, j):
            return state[t, f, 8 * j : 8 * j + 8, :] if j < 4 else halo[t, f]

        def before(f, j):
            if t == 1:
                return state[0, f, 8 * j : 8 * j + 8, :] if j < 4 else halo[0, f]
            return prev[f, 8 * j : 8 * j + 8, :] if j < 4 else prev_halo[f]

        last = residual_tile(load, 4, before)
        held = last
        for j in range(4):
            now = residual_tile(load, j, before)
            for f in range(3):
                res[f * R + 8 * j : f * R + 8 * j + 8, :] = pltpu.roll(
                    jnp.where(sub8 < 4, now[f], held[f]), 4, 0
                )
            held = now
        for f in range(3):
            res[f * R + 32 : f * R + 40, :] = pltpu.roll(
                jnp.where(sub8 < 4, last[f], held[f]), 4, 0
            )
        for b in range(cols // 128):
            block = res[:, 128 * b : 128 * b + 128].T
            for i in range(128 // width):
                send[t, b * (128 // width) + i, 0:width, :] = block[width * i : width * i + width]

        def margin(p, carry):
            right, left = lax.rem(p + 1, ntm), lax.rem(p + ntm - 1, ntm)
            send[t, p, width : width + 8, :] = jnp.where(
                sub8 < 4, send[t, right, 0:8, :], send[t, left, width - 8 : width, :]
            )
            return carry

        lax.fori_loop(0, ntm, margin, 0)

        def go(k, carry):
            in_copy(t, lax.rem(me + k, ntm), 2 * me + t).start()
            return carry

        lax.fori_loop(1, ntm, go, 0)
        s_buf[2 * me + t] = send[t, me]

    normal[0].wait_recv()
    normal[1].wait_recv()
    step_out(1)
    for copy in normal[2:]:
        copy.wait_recv()
    step_out(0)

    for copy in normal:
        copy.wait_send()

    def landed(k, carry):
        p = lax.rem(me + k, ntm)
        for t in (1, 0):
            copy = in_copy(t, p, 2 * p + t)
            copy.wait_send()
            copy.wait_recv()
        return carry

    lax.fori_loop(1, ntm, landed, 0)

    lane = lax.broadcasted_iota(jnp.int32, (8, 128), 1)
    field = [(lane >= f * R) & (lane < (f + 1) * R) for f in range(3)]
    lanes = [m.astype(f32) for m in field]
    rows = width + 8

    def wide(x):
        return jnp.concatenate([x] * (rows // 8), axis=0)

    is0 = wide(lanes[0]) > 0.5
    k_col = wide(0.25 * (lanes[0] + lanes[1]))
    k_row = wide(0.25 * (lanes[0] + lanes[2]))
    k_a = wide(0.3 * lanes[1])
    k_b = wide(-0.3 * lanes[2])

    def lhs(s, y):
        a = pltpu.roll(y, 128 - R, 1)
        b = pltpu.roll(y, R, 1)
        a2 = pltpu.roll(y, 128 - 2 * R, 1)
        b2 = pltpu.roll(y, 2 * R, 1)
        scaled = 0.2 * y
        col = k_col * jnp.where(is0, a, b)
        row = k_row * jnp.where(is0, a2, b2)
        right = pltpu.roll(scaled - col, rows - 1, 0)
        left = pltpu.roll(scaled + col, 1, 0)
        north = pltpu.roll(scaled - row, 127, 1)
        south = pltpu.roll(scaled + row, 1, 1)
        return ((s + k_a * a) + (right + left)) + ((north + south) + k_b * b)

    weights = sweep_weights()
    closing = ALPHA / (1.0 - ALPHA * A**steps)
    zero = jnp.zeros((rows, 128), f32)

    def first(n, h):
        h = A * (s_buf[n] + h)
        y_buf[n] = weights[0] * h
        return h

    h = lax.fori_loop(0, steps, first, zero, unroll=4)
    wrap = (A * weights[0] * closing) * h
    for m in range(1, SWEEPS):

        def sweep(n, carry, m=m):
            h, wrap = carry
            y = y_buf[n] + wrap
            h = A * (lhs(s_buf[n], y) + h)
            y_buf[n] = (1.0 - weights[m]) * y + weights[m] * h
            return h, A * wrap

        h, _ = lax.fori_loop(0, steps, sweep, (zero, wrap), unroll=2)
        wrap = (A * weights[m] * closing) * h

    def back_copy(d, slot):
        return pltpu.make_async_remote_copy(
            src_ref=corr.at[d],
            dst_ref=back.at[slot],
            send_sem=back_send.at[d],
            recv_sem=back_recv.at[slot],
            device_id=(d, sp),
            device_id_type=MESH,
        )

    def finish(d, wrap):
        for t in range(2):
            corr[d, t] = pltpu.roll(y_buf[2 * d + t, 0:width, :] + wrap, 124, 1)
            wrap = A * wrap
        return wrap

    lax.fori_loop(0, ntm, finish, wrap[0:width, :])

    def back_go(k, carry):
        back_copy(lax.rem(me + k, ntm), me).start()
        return carry

    lax.fori_loop(1, ntm, back_go, 0)
    back[me] = corr[me]

    def back_landed(k, carry):
        p = lax.rem(me + k, ntm)
        copy = back_copy(p, p)
        copy.wait_send()
        copy.wait_recv()
        return carry

    lax.fori_loop(1, ntm, back_landed, 0)

    for t in range(2):
        for b in range(cols // 128):
            per = 128 // width
            block = jnp.concatenate([back[b * per + i, t] for i in range(per)], axis=0).T
            for f in range(3):
                out[t, f, :, 128 * b : 128 * b + 128] = (
                    state[t, f, :, 128 * b : 128 * b + 128] - block[f * R : f * R + 32, :]
                )


def solution(mesh):
    ntm, nsp = mesh.shape["tm"], mesh.shape["space"]

    def on_device(state, initial):
        cols = state.shape[3]
        width = cols // ntm
        vmem = pltpu.VMEM
        return pl.pallas_call(
            functools.partial(kernel, ntm, nsp),
            out_shape=jax.ShapeDtypeStruct(state.shape, f32),
            in_specs=[pl.BlockSpec(memory_space=vmem)] * 2,
            out_specs=pl.BlockSpec(memory_space=vmem),
            scratch_shapes=[
                vmem((2, 3, 8, cols), f32),
                vmem((3, 32, cols), f32),
                vmem((3, 8, cols), f32),
                vmem((128, cols), f32),
                vmem((2, ntm, width + 8, 128), f32),
                vmem((2 * ntm, width + 8, 128), f32),
                vmem((2 * ntm, width + 8, 128), f32),
                vmem((ntm, 2, width, 128), f32),
                vmem((ntm, 2, width, 128), f32),
                pltpu.SemaphoreType.DMA((5,)),
                pltpu.SemaphoreType.DMA((5,)),
                pltpu.SemaphoreType.DMA((2, ntm)),
                pltpu.SemaphoreType.DMA((2, ntm)),
                pltpu.SemaphoreType.DMA((ntm,)),
                pltpu.SemaphoreType.DMA((ntm,)),
            ],
            compiler_params=pltpu.CompilerParams(
                collective_id=0, has_side_effects=True, vmem_limit_bytes=48 << 20
            ),
        )(state, initial)

    return jax.shard_map(
        on_device,
        mesh=mesh,
        in_specs=(P("tm", None, "space", None), P(None, "space", None)),
        out_specs=P("tm", None, "space", None),
        check_vma=False,
    )
```

time: 182 us -> 74.2 us (0.41)
  the two profiles are of different devices: /device:TPU:1 before, /device:TPU:69 now
where the time goes in v1:
time: 74.2 us; the launch traced here: 74 us
  Pallas kernels  71 us (96%)
  local copies, waits for them, and re-layouts  3.01 us (4%)
    pallas_call x1, Pallas kernels, on_device(): pl.pallas_call(functools.partial(kernel, ntm, nsp), out_shape=jax.ShapeDt...  71 us
    unnamed x5, local copies, waits for them, and re-layouts  3.01 us

profile of v1, /device:TPU:69, one launch (start us, length us, event | category | flops | bytes accessed | tf_op | source)
XLA Modules:
  0.0 74.0 jit_solution(10085765087313929129)
XLA Ops:
  0.0 0.0 copy-start
  0.0 1.1 %copy-done = f32[2,3,32,1024]{3,2,1,0:T(8,128)S(1)} copy-done((f32[2,3,32,1024]{3,2,1,0:T(8,128)S(1)}, f32[2,3,32,1024]{3,2,1,0:T(8,128)}, u32[]{:S(2)}) %copy-start) | copy-done | bytes 786456
  1.1 0.0 copy-start.1
  1.1 1.0 %copy-done.1 = f32[3,32,1024]{2,1,0:T(8,128)S(1)} copy-done((f32[3,32,1024]{2,1,0:T(8,128)S(1)}, f32[3,32,1024]{2,1,0:T(8,128)}, u32[]{:S(2)}) %copy-start.1) | copy-done | bytes 393240
  2.1 71.0 %shard_map.28 = f32[2,3,32,1024]{3,2,1,0:T(8,128)S(1)} custom-call(f32[2,3,32,1024]{3,2,1,0:T(8,128)S(1)} %copy-done, f32[3,32,1024]{2,1,0:T(8,128)S(1)} %copy-done.1), custom_call_target="tpu_custom_call" | custom-call | tf_op jit(solution)/shard_map/pallas_call | solution.py:318
  73.1 0.9 %copy.4 = f32[2,3,32,1024]{3,2,1,0:T(8,128)} copy(f32[2,3,32,1024]{3,2,1,0:T(8,128)S(1)} %shard_map.28) | data formatting | bytes 1572864
Async XLA Ops:
  0.0 1.1 %copy-start = (f32[2,3,32,1024]{3,2,1,0:T(8,128)S(1)}, f32[2,3,32,1024]{3,2,1,0:T(8,128)}, u32[]{:S(2)}) copy-start(f32[2,3,32,1024]{3,2,1,0:T(8,128)} %state.1) | copy-start | bytes 2359300
  1.1 1.0 %copy-start.1 = (f32[3,32,1024]{2,1,0:T(8,128)S(1)}, f32[3,32,1024]{2,1,0:T(8,128)}, u32[]{:S(2)}) copy-start(f32[3,32,1024]{2,1,0:T(8,128)} %initial.1) | copy-start | bytes 1179652

commit v2 on v1

--- a/solution.py
+++ b/solution.py
@@ -3,6 +3,7 @@
 
 import jax
 import jax.numpy as jnp
+import numpy as np
 from jax import lax
 from jax.experimental import pallas as pl
 from jax.experimental.pallas import tpu as pltpu
@@ -11,6 +12,7 @@
 SWEEPS = 4
 ALPHA = 0.1
 A = 1.0 / 1.8
+CHUNK = 8
 R = 40
 MESH = pl.DeviceIdType.MESH
 f32 = jnp.float32
@@ -20,6 +22,33 @@
     return [
         1.0 / (1.15 - 0.85 * math.cos(math.pi * (2 * m + 1) / (2 * SWEEPS))) for m in range(SWEEPS)
     ]
+
+
+def stencil_table():
+    table = np.zeros((3, 128, 128), np.float32)
+    for f in range(3):
+        for r in range(R):
+            here = f * R + r
+            table[1:, here, here] = 4.0
+            for step in (-1, 1):
+                if 0 <= r + step < R:
+                    table[0, here + step, here] = 4.0
+                    if f != 1:
+                        table[0, (2 - f) * R + r + step, here] = -5.0 * step
+    for r in range(R):
+        table[0, 2 * R + r, R + r] = 6.0
+        table[0, R + r, 2 * R + r] = -6.0
+        table[1, R + r, r] = table[1, r, R + r] = -5.0
+        table[2, R + r, r] = table[2, r, R + r] = 5.0
+    one = np.concatenate(list(table), axis=1)
+    return jnp.asarray(np.concatenate([one, one], axis=0), jnp.bfloat16)
+
+
+def far_first(shape):
+    span = [[(d, min(d, n - d)) for d in range(n)] for n in shape]
+    every = [(x, z, c) for x in span[0] for z in span[1] for c in span[2]]
+    every.sort(key=lambda d: -(d[0][1] + d[1][1]))
+    return [tuple(a[0] for a in d) for d in every if any(a[0] for a in d)]
 
 
 def residual_tile(load, j, before):
@@ -56,9 +85,12 @@
 def kernel(
     ntm,
     nsp,
+    state_hbm,
+    initial,
+    stencil_hbm,
+    out,
     state,
-    initial,
-    out,
+    stencil,
     halo,
     prev,
     prev_halo,
@@ -74,12 +106,20 @@
     in_recv,
     back_send,
     back_recv,
+    load_sem,
+    fade,
 ):
     me = lax.axis_index("tm")
     sp = lax.axis_index("space")
     nxt, prv = lax.rem(me + 1, ntm), lax.rem(me + ntm - 1, ntm)
     up, dn = lax.rem(sp + 1, nsp), lax.rem(sp + nsp - 1, nsp)
     cols = state.shape[3]
+    shape = (4, ntm // 8, 2)
+    x, z, c = lax.div(me, 2 * shape[1]), lax.rem(lax.div(me, 2), shape[1]), lax.rem(me, 2)
+    others = [
+        (lax.rem(x + dx, shape[0]) * shape[1] + lax.rem(z + dz, shape[1])) * 2 + lax.rem(c + dc, 2)
+        for dx, dz, dc in far_first(shape)
+    ]
     steps = 2 * ntm
     width = cols // ntm
     sub8 = lax.broadcasted_iota(jnp.int32, (8, 1), 0)
@@ -96,6 +136,11 @@
         return carry
 
     lax.fori_loop(1, ntm, greet, 0)
+    loads = [
+        pltpu.make_async_copy(state_hbm.at[t], state.at[t], load_sem.at[t]) for t in (1, 0)
+    ] + [pltpu.make_async_copy(stencil_hbm, stencil, load_sem.at[2])]
+    for copy in loads:
+        copy.start()
     pl.semaphore_wait(barrier, ntm - 1 + len(around))
 
     def exchange(i, src, dst, device):
@@ -113,8 +158,8 @@
 
     def edges():
         return [
-            exchange(0, state.at[:, :, low], halo.at[:, :, low], (me, dn)),
-            exchange(1, state.at[:, :, rows_hi], halo.at[:, :, high], (me, up)),
+            exchange(0, state_hbm.at[:, :, low], halo.at[:, :, low], (me, dn)),
+            exchange(1, state_hbm.at[:, :, rows_hi], halo.at[:, :, high], (me, up)),
         ]
 
     def handed(last):
@@ -124,7 +169,7 @@
             exchange(4, last.at[:, rows_hi], prev_halo.at[:, high], (nxt, up)),
         ]
 
-    normal = edges() + handed(state.at[1])
+    normal = edges() + handed(state_hbm.at[1])
     for copy in normal[:2]:
         copy.start()
 
@@ -186,13 +231,16 @@
 
         lax.fori_loop(0, ntm, margin, 0)
 
-        def go(k, carry):
-            in_copy(t, lax.rem(me + k, ntm), 2 * me + t).start()
-            return carry
-
-        lax.fori_loop(1, ntm, go, 0)
+        for p in others:
+            in_copy(t, p, 2 * me + t).start()
         s_buf[2 * me + t] = send[t, me]
 
+    gain = jnp.float32(1.0)
+    for n in range(ntm):
+        fade[n] = gain
+        gain = gain * (A * A)
+    for copy in loads:
+        copy.wait()
     normal[0].wait_recv()
     normal[1].wait_recv()
     step_out(1)
@@ -213,56 +261,47 @@
 
     lax.fori_loop(1, ntm, landed, 0)
 
-    lane = lax.broadcasted_iota(jnp.int32, (8, 128), 1)
-    field = [(lane >= f * R) & (lane < (f + 1) * R) for f in range(3)]
-    lanes = [m.astype(f32) for m in field]
     rows = width + 8
-
-    def wide(x):
-        return jnp.concatenate([x] * (rows // 8), axis=0)
-
-    is0 = wide(lanes[0]) > 0.5
-    k_col = wide(0.25 * (lanes[0] + lanes[1]))
-    k_row = wide(0.25 * (lanes[0] + lanes[2]))
-    k_a = wide(0.3 * lanes[1])
-    k_b = wide(-0.3 * lanes[2])
-
-    def lhs(s, y):
-        a = pltpu.roll(y, 128 - R, 1)
-        b = pltpu.roll(y, R, 1)
-        a2 = pltpu.roll(y, 128 - 2 * R, 1)
-        b2 = pltpu.roll(y, 2 * R, 1)
-        scaled = 0.2 * y
-        col = k_col * jnp.where(is0, a, b)
-        row = k_row * jnp.where(is0, a2, b2)
-        right = pltpu.roll(scaled - col, rows - 1, 0)
-        left = pltpu.roll(scaled + col, 1, 0)
-        north = pltpu.roll(scaled - row, 127, 1)
-        south = pltpu.roll(scaled + row, 1, 1)
-        return ((s + k_a * a) + (right + left)) + ((north + south) + k_b * b)
-
     weights = sweep_weights()
     closing = ALPHA / (1.0 - ALPHA * A**steps)
     zero = jnp.zeros((rows, 128), f32)
 
-    def first(n, h):
-        h = A * (s_buf[n] + h)
-        y_buf[n] = weights[0] * h
+    def first(i, h):
+        for q in range(CHUNK):
+            n = CHUNK * i + q
+            h = A * (s_buf[n] + h)
+            y_buf[n] = (0.05 * weights[0]) * h
         return h
 
-    h = lax.fori_loop(0, steps, first, zero, unroll=4)
-    wrap = (A * weights[0] * closing) * h
+    h = lax.fori_loop(0, steps // CHUNK, first, zero)
+    wrap = (0.05 * A * weights[0] * closing) * h
     for m in range(1, SWEEPS):
-
-        def sweep(n, carry, m=m):
+        keep, gain = 1.0 - weights[m], 0.05 * weights[m]
+        if m == SWEEPS - 1:
+            keep, gain = 20.0 * keep, 20.0 * gain
+
+        def sweep(i, carry, keep=keep, gain=gain):
             h, wrap = carry
-            y = y_buf[n] + wrap
-            h = A * (lhs(s_buf[n], y) + h)
-            y_buf[n] = (1.0 - weights[m]) * y + weights[m] * h
-            return h, A * wrap
-
-        h, _ = lax.fori_loop(0, steps, sweep, (zero, wrap), unroll=2)
-        wrap = (A * weights[m] * closing) * h
+            ys = []
+            for q in range(CHUNK):
+                ys.append(y_buf[CHUNK * i + q] + wrap)
+                wrap = A * wrap
+            y = jnp.concatenate(ys, axis=0)
+            high_part = y.astype(jnp.bfloat16)
+            low_part = (y - high_part.astype(f32)).astype(jnp.bfloat16)
+            parts = jnp.concatenate([high_part, low_part], axis=1)
+            mixed = jnp.dot(parts, stencil[...], preferred_element_type=f32)
+            for q in range(CHUNK):
+                n = CHUNK * i + q
+                part = mixed[rows * q : rows * q + rows]
+                own, east, west = part[:, :128], part[:, 128:256], part[:, 256:]
+                beside = pltpu.roll(east, rows - 1, 0) + pltpu.roll(west, 1, 0)
+                h = A * (((s_buf[n] + own) + beside) + h)
+                y_buf[n] = keep * ys[q] + gain * h
+            return h, wrap
+
+        h, _ = lax.fori_loop(0, steps // CHUNK, sweep, (zero, wrap))
+        wrap = (gain * A * closing) * h
 
     def back_copy(d, slot):
         return pltpu.make_async_remote_copy(
@@ -274,19 +313,38 @@
             device_id_type=MESH,
         )
 
-    def finish(d, wrap):
-        for t in range(2):
-            corr[d, t] = pltpu.roll(y_buf[2 * d + t, 0:width, :] + wrap, 124, 1)
-            wrap = A * wrap
-        return wrap
-
-    lax.fori_loop(0, ntm, finish, wrap[0:width, :])
-
-    def back_go(k, carry):
-        back_copy(lax.rem(me + k, ntm), me).start()
-        return carry
-
-    lax.fori_loop(1, ntm, back_go, 0)
+    slot_lane = lax.broadcasted_iota(jnp.int32, (width, 128), 1)
+    parts = [slot_lane < 32, slot_lane < 64, slot_lane < 96]
+    wrap = wrap[0:width, :]
+
+    def finish(d):
+        closed = wrap * fade[d]
+        one = y_buf[2 * d, 0:width, :] + closed
+        two = y_buf[2 * d + 1, 0:width, :] + A * closed
+        moved = [pltpu.roll(one, 124 - 8 * f, 1) for f in range(3)]
+        corr[d, 0:width, :] = jnp.where(
+            parts[0],
+            moved[0],
+            jnp.where(parts[1], moved[1], jnp.where(parts[2], moved[2], pltpu.roll(two, 92, 1))),
+        )
+        half = width // 2
+        top, end = two[0:half], two[half:width]
+        corr[d, width : width + half, :] = jnp.where(
+            parts[0][0:half],
+            pltpu.roll(top, 84, 1),
+            jnp.where(
+                parts[1][0:half],
+                pltpu.roll(top, 76, 1),
+                jnp.where(parts[2][0:half], pltpu.roll(end, 20, 1), pltpu.roll(end, 12, 1)),
+            ),
+        )
+
+    for i, d in enumerate(others):
+        finish(d)
+        if i > 0:
+            back_copy(others[i - 1], me).start()
+    finish(me)
+    back_copy(others[-1], me).start()
     back[me] = corr[me]
 
     def back_landed(k, carry):
@@ -298,14 +356,20 @@
 
     lax.fori_loop(1, ntm, back_landed, 0)
 
-    for t in range(2):
-        for b in range(cols // 128):
-            per = 128 // width
-            block = jnp.concatenate([back[b * per + i, t] for i in range(per)], axis=0).T
-            for f in range(3):
-                out[t, f, :, 128 * b : 128 * b + 128] = (
-                    state[t, f, :, 128 * b : 128 * b + 128] - block[f * R : f * R + 32, :]
-                )
+    per, half = 128 // width, width // 2
+    for b in range(cols // 128):
+        here = pl.ds(128 * b, 128)
+        first_part = jnp.concatenate([back[b * per + i, 0:width] for i in range(per)], axis=0).T
+        rest = []
+        for i in range(per):
+            piece = back[b * per + i, width : width + half]
+            rest += [piece, pltpu.roll(piece, 64, 1)]
+        second_part = jnp.concatenate(rest, axis=0).T
+        for f in range(3):
+            out[0, f, :, here] = state[0, f, :, here] - first_part[32 * f : 32 * f + 32]
+        out[1, 0, :, here] = state[1, 0, :, here] - first_part[96:128]
+        for f in (1, 2):
+            out[1, f, :, here] = state[1, f, :, here] - second_part[32 * f - 32 : 32 * f]
 
 
 def solution(mesh):
@@ -318,9 +382,11 @@
         return pl.pallas_call(
             functools.partial(kernel, ntm, nsp),
             out_shape=jax.ShapeDtypeStruct(state.shape, f32),
-            in_specs=[pl.BlockSpec(memory_space=vmem)] * 2,
+            in_specs=[pl.BlockSpec(memory_space=pl.ANY)] * 3,
             out_specs=pl.BlockSpec(memory_space=vmem),
             scratch_shapes=[
+                vmem(state.shape, f32),
+                vmem((256, 384), jnp.bfloat16),
                 vmem((2, 3, 8, cols), f32),
                 vmem((3, 32, cols), f32),
                 vmem((3, 8, cols), f32),
@@ -328,19 +394,21 @@
                 vmem((2, ntm, width + 8, 128), f32),
                 vmem((2 * ntm, width + 8, 128), f32),
                 vmem((2 * ntm, width + 8, 128), f32),
-                vmem((ntm, 2, width, 128), f32),
-                vmem((ntm, 2, width, 128), f32),
+                vmem((ntm, width + width // 2, 128), f32),
+                vmem((ntm, width + width // 2, 128), f32),
                 pltpu.SemaphoreType.DMA((5,)),
                 pltpu.SemaphoreType.DMA((5,)),
                 pltpu.SemaphoreType.DMA((2, ntm)),
                 pltpu.SemaphoreType.DMA((2, ntm)),
                 pltpu.SemaphoreType.DMA((ntm,)),
                 pltpu.SemaphoreType.DMA((ntm,)),
+                pltpu.SemaphoreType.DMA((3,)),
+                pltpu.SMEM((ntm,), f32),
             ],
             compiler_params=pltpu.CompilerParams(
-                collective_id=0, has_side_effects=True, vmem_limit_bytes=48 << 20
+                collective_id=0, has_side_effects=True, vmem_limit_bytes=60 << 20
             ),
-        )(state, initial)
+        )(state, initial, stencil_table())
 
     return jax.shard_map(
         on_device,

time: 74.2 us -> 55.1 us (0.74)
  the two profiles are of different devices: /device:TPU:69 before, /device:TPU:1 now
where the time goes in v2:
time: 55.1 us; the launch traced here: 54.9 us
  Pallas kernels  52.8 us (96%)
  local copies, waits for them, and re-layouts  2.09 us (4%)
    pallas_call x1, Pallas kernels, on_device(): pl.pallas_call(functools.partial(kernel, ntm, nsp), out_shape=jax.ShapeDt...  52.8 us
    unnamed x1, local copies, waits for them, and re-layouts  2.09 us

profile of v2, /device:TPU:1, one launch (start us, length us, event | category | flops | bytes accessed | tf_op | source)
XLA Modules:
  0.0 54.9 jit_solution(348494779899491803)
XLA Ops:
  0.0 52.8 %shard_map.37 = f32[2,3,32,1024]{3,2,1,0:T(8,128)} custom-call(f32[2,3,32,1024]{3,2,1,0:T(8,128)} %state_hbm.1, f32[3,32,1024]{2,1,0:T(8,128)} %initial.1, bf16[256,384]{1,0:T(8,128)(2,1)} %constant.2.clone.stencil_hbm), custom_call_target="tpu_custom_call" | custom-call | tf_op jit(solution)/shard_map/pallas_call | solution.py:382
  52.8 2.1 %copy.5 = f32[2,3,32,1024]{3,2,1,0:T(8,128)} copy(f32[2,3,32,1024]{3,2,1,0:T(8,128)} %shard_map.37) | data formatting | bytes 1572864

commit v3 on v2

v3 whole, which is shorter than its diff:
```python
import functools
import math

import jax
import jax.numpy as jnp
import numpy as np
from jax import lax
from jax.experimental import pallas as pl
from jax.experimental.pallas import tpu as pltpu
from jax.sharding import PartitionSpec as P

SWEEPS = 4
ALPHA = 0.1
A = 1.0 / 1.8
CHUNK = 32
PARTS = 1
R = 40
MESH = pl.DeviceIdType.MESH
f32 = jnp.float32


def sweep_weights():
    return [
        1.0 / (1.15 - 0.85 * math.cos(math.pi * (2 * m + 1) / (2 * SWEEPS))) for m in range(SWEEPS)
    ]


def stencil_table():
    table = np.zeros((2, 128, 128), np.float32)
    for f in range(3):
        for r in range(R):
            here = f * R + r
            for step in (-1, 1):
                if 0 <= r + step < R:
                    table[0, here + step, here] = 4.0
                    if f != 1:
                        table[0, (2 - f) * R + r + step, here] = -5.0 * step
    for r in range(R):
        table[0, 2 * R + r, R + r] = 6.0
        table[0, R + r, 2 * R + r] = -6.0
        table[1, R + r, r] = table[1, r, R + r] = -5.0
    one = np.concatenate(list(table), axis=1)
    return jnp.asarray(np.concatenate([one, one], axis=0), jnp.bfloat16)


def far_first(shape):
    span = [[(d, min(d, n - d)) for d in range(n)] for n in shape]
    every = [(x, z, c) for x in span[0] for z in span[1] for c in span[2]]
    every.sort(key=lambda d: -(d[0][1] + d[1][1]))
    return [tuple(a[0] for a in d) for d in every if any(a[0] for a in d)]


def residual_tile(load, j, before):
    sub = lax.broadcasted_iota(jnp.int32, (8, 1), 0)

    def near(f):
        here, after, ahead = load(f, j), load(f, (j + 1) % 5), load(f, (j + 4) % 5)
        cols = here.shape[1]
        north = pltpu.roll(jnp.where(sub == 0, after, here), 7, 0)
        south = pltpu.roll(jnp.where(sub == 7, ahead, here), 1, 0)
        east = pltpu.roll(here, cols - 1, 1)
        west = pltpu.roll(here, 1, 1)
        return here, east, west, north, south

    e, ee, ew, en, es = near(0)
    u, ue, uw, un, us = near(1)
    v, ve, vw, vn, vs = near(2)
    mass = 0.25 * (
        ((1.0 + ee) * ue - (1.0 + ew) * uw) + ((1.0 + en) * vn - (1.0 + es) * vs)
    ) - 0.2 * (ee + ew + en + es - 4.0 * e)
    east = (
        0.25 * (u * (ue - uw) + v * (un - us) + (ee - ew))
        - 0.3 * v
        - 0.2 * (ue + uw + un + us - 4.0 * u)
    )
    north = (
        0.25 * (u * (ve - vw) + v * (vn - vs) + (en - es))
        + 0.3 * u
        - 0.2 * (ve + vw + vn + vs - 4.0 * v)
    )
    return [x - before(f, j) + t for f, (x, t) in enumerate(((e, mass), (u, east), (v, north)))]


def kernel(
    ntm,
    nsp,
    state_hbm,
    initial,
    stencil_hbm,
    out,
    state,
    stencil,
    halo,
    prev,
    prev_halo,
    res,
    send,
    s_buf,
    y_buf,
    corr,
    back,
    ex_send,
    ex_recv,
    in_send,
    in_recv,
    back_send,
    back_recv,
    load_sem,
    fade,
):
    me = lax.axis_index("tm")
    sp = lax.axis_index("space")
    nxt, prv = lax.rem(me + 1, ntm), lax.rem(me + ntm - 1, ntm)
    up, dn = lax.rem(sp + 1, nsp), lax.rem(sp + nsp - 1, nsp)
    cols = state.shape[3]
    shape = (4, ntm // 8, 2)
    x, z, c = lax.div(me, 2 * shape[1]), lax.rem(lax.div(me, 2), shape[1]), lax.rem(me, 2)
    others = [
        (lax.rem(x + dx, shape[0]) * shape[1] + lax.rem(z + dz, shape[1])) * 2 + lax.rem(c + dc, 2)
        for dx, dz, dc in far_first(shape)
    ]
    steps = 2 * ntm
    width = cols // ntm
    sub8 = lax.broadcasted_iota(jnp.int32, (8, 1), 0)

    def clear(n, carry):
        s_buf[n, 0:8, :] = jnp.zeros((8, 128), f32)
        s_buf[n, 8 + width : 16 + width, :] = jnp.zeros((8, 128), f32)
        return carry

    lax.fori_loop(0, steps, clear, 0, unroll=8)
    barrier = pltpu.get_barrier_semaphore()
    around = [(me, up), (me, dn), (nxt, up), (nxt, dn), (prv, up), (prv, dn)]
    for other in around:
        pl.semaphore_signal(barrier, inc=1, device_id=other, device_id_type=MESH)

    def greet(k, carry):
        pl.semaphore_signal(
            barrier, inc=1, device_id=(lax.rem(me + k, ntm), sp), device_id_type=MESH
        )
        return carry

    lax.fori_loop(1, ntm, greet, 0)
    loads = [
        pltpu.make_async_copy(state_hbm.at[t], state.at[t], load_sem.at[t]) for t in (1, 0)
    ] + [pltpu.make_async_copy(stencil_hbm, stencil, load_sem.at[2])]
    for copy in loads:
        copy.start()
    pl.semaphore_wait(barrier, ntm - 1 + len(around))

    def exchange(i, src, dst, device):
        return pltpu.make_async_remote_copy(
            src_ref=src,
            dst_ref=dst,
            send_sem=ex_send.at[i],
            recv_sem=ex_recv.at[i],
            device_id=device,
            device_id_type=MESH,
        )

    low, high = pl.ds(0, 4), pl.ds(4, 4)
    rows_hi = pl.ds(28, 4)

    def edges(t):
        return [
            exchange(2 * t, state_hbm.at[t, :, low], halo.at[t, :, low], (me, dn)),
            exchange(2 * t + 1, state_hbm.at[t, :, rows_hi], halo.at[t, :, high], (me, up)),
        ]

    def handed(last):
        return [
            exchange(4, last, prev, (nxt, sp)),
            exchange(5, last.at[:, low], prev_halo.at[:, low], (nxt, dn)),
            exchange(6, last.at[:, rows_hi], prev_halo.at[:, high], (nxt, up)),
        ]

    normal = edges(0) + edges(1) + handed(state_hbm.at[1])
    for copy in normal[:4]:
        copy.start()

    @pl.when(me != ntm - 1)
    def _():
        for copy in normal[4:]:
            copy.start()

    @pl.when(me == ntm - 1)
    def _():
        for copy in handed(initial):
            copy.start()

    own = width // PARTS

    def in_copy(t, i, p, slot):
        start = 5 if i == 0 else 12 + own * i
        end = 11 + width if t == 1 or i == PARTS - 1 else 12 + own * (i + 1)
        rows = pl.ds(start, end - start)
        return pltpu.make_async_remote_copy(
            src_ref=send.at[t, p, rows],
            dst_ref=s_buf.at[slot, rows],
            send_sem=in_send.at[t, i, p],
            recv_sem=in_recv.at[t, i, lax.div(slot, 2)],
            device_id=(p, sp),
            device_id_type=MESH,
        )

    res[3 * R :, :] = jnp.zeros((res.shape[0] - 3 * R, cols), f32)

    def step_out(t):
        def load(f, j):
            return state[t, f, 8 * j : 8 * j + 8, :] if j < 4 else halo[t, f]

        def before(f, j):
            if t == 1:
                return state[0, f, 8 * j : 8 * j + 8, :] if j < 4 else halo[0, f]
            return prev[f, 8 * j : 8 * j + 8, :] if j < 4 else prev_halo[f]

        last = residual_tile(load, 4, before)
        held = last
        for j in range(4):
            now = residual_tile(load, j, before)
            for f in range(3):
                res[f * R + 8 * j : f * R + 8 * j + 8, :] = pltpu.roll(
                    jnp.where(sub8 < 4, now[f], held[f]), 4, 0
                )
            held = now
        for f in range(3):
            res[f * R + 32 : f * R + 40, :] = pltpu.roll(
                jnp.where(sub8 < 4, last[f], held[f]), 4, 0
            )
        for b in range(cols // 128):
            block = res[:, 128 * b : 128 * b + 128].T
            for i in range(128 // width):
                send[t, b * (128 // width) + i, 8 : 8 + width, :] = block[width * i : width * i + width]

        def margin(p, carry):
            right, left = lax.rem(p + 1, ntm), lax.rem(p + ntm - 1, ntm)
            send[t, p, 4:8, :] = send[t, left, 4 + width : 8 + width, :]
            send[t, p, 8 + width : 12 + width, :] = send[t, right, 8:12, :]
            return carry

        lax.fori_loop(0, ntm, margin, 0)

    def go(t, i):
        for p in others:
            in_copy(t, i, p, 2 * me + t).start()

    gain = jnp.float32(1.0)
    for n in range(ntm):
        fade[n] = gain
        gain = gain * (A * A)
    for copy in loads:
        copy.wait()
    for copy in normal[:4]:
        copy.wait_recv()
    step_out(1)
    go(1, 0)
    for copy in normal[4:]:
        copy.wait_recv()
    step_out(0)
    go(0, 0)
    for i in range(1, PARTS):
        for p in others:
            in_copy(0, i - 1, p, 2 * me).wait_send()
            in_copy(0, i, p, 2 * me).start()
    for t in range(2):
        s_buf[2 * me + t] = send[t, me]

    def landed(i):
        def one(k, carry):
            p = lax.rem(me + k, ntm)
            if i == 0:
                in_copy(1, 0, p, 2 * p + 1).wait_recv()
            in_copy(0, i, p, 2 * p).wait_recv()
            return carry

        lax.fori_loop(1, ntm, one, 0)

    rows = own + 8
    weights = sweep_weights()
    closing = ALPHA / (1.0 - ALPHA * A**steps)
    zero = jnp.zeros((rows, 128), f32)

    def solve(i):
        start = 8 + own * i

        def rhs(n):
            after = s_buf[n, start + own : start + own + 8, :]
            ahead = s_buf[n, start - 8 : start, :]
            return jnp.concatenate(
                [s_buf[n, start : start + own, :], jnp.where(sub8 < 4, after, ahead)], axis=0
            )

        def first(k, h):
            for q in range(CHUNK):
                n = CHUNK * k + q
                h = A * (rhs(n) + h)
                y_buf[n] = (0.05 * weights[0]) * h
            return h

        h = lax.fori_loop(0, steps // CHUNK, first, zero)
        wrap = (0.05 * A * weights[0] * closing) * h
        for m in range(1, SWEEPS):
            keep, gain = 1.0 - weights[m], 0.05 * weights[m]
            if m == SWEEPS - 1:
                keep, gain = 20.0 * keep, 20.0 * gain

            def sweep(k, carry, keep=keep, gain=gain):
                h, wrap = carry
                ys = []
                for q in range(CHUNK):
                    ys.append(y_buf[CHUNK * k + q] + wrap)
                    wrap = A * wrap
                y = jnp.concatenate(ys, axis=0)
                high_part = y.astype(jnp.bfloat16)
                low_part = (y - high_part.astype(f32)).astype(jnp.bfloat16)
                both = jnp.concatenate([high_part, low_part], axis=1)
                mixed = jnp.dot(both, stencil[...], preferred_element_type=f32)
                for q in range(CHUNK):
                    n = CHUNK * k + q
                    part = mixed[rows * q : rows * q + rows]
                    here, cross, even = part[:, :128], part[:, 128:], 4.0 * ys[q]
                    beside = pltpu.roll(even + cross, rows - 1, 0) + pltpu.roll(even - cross, 1, 0)
                    h = A * (((rhs(n) + here) + beside) + h)
                    y_buf[n] = keep * ys[q] + gain * h
                return h, wrap

            h, _ = lax.fori_loop(0, steps // CHUNK, sweep, (zero, wrap))
            wrap = (gain * A * closing) * h
        return wrap[0:own, :]

    def back_copy(i, d, slot):
        return pltpu.make_async_remote_copy(
            src_ref=corr.at[d, i],
            dst_ref=back.at[slot, i],
            send_sem=back_send.at[i, d],
            recv_sem=back_recv.at[i, slot],
            device_id=(d, sp),
            device_id_type=MESH,
        )

    lane = lax.broadcasted_iota(jnp.int32, (own, 128), 1)
    below = [lane < 32, lane < 64, lane < 96]
    half = own // 2

    def finish(i, d, wrap):
        closed = wrap * fade[d]
        one = y_buf[2 * d, 0:own, :] + closed
        two = y_buf[2 * d + 1, 0:own, :] + A * closed
        moved = [pltpu.roll(one, 124 - 8 * f, 1) for f in range(3)]
        corr[d, i, 0:own, :] = jnp.where(
            below[0],
            moved[0],
            jnp.where(below[1], moved[1], jnp.where(below[2], moved[2], pltpu.roll(two, 92, 1))),
        )
        top, end = two[0:half], two[half:own]
        corr[d, i, own : own + half, :] = jnp.where(
            below[0][0:half],
            pltpu.roll(top, 84, 1),
            jnp.where(
                below[1][0:half],
                pltpu.roll(top, 76, 1),
                jnp.where(below[2][0:half], pltpu.roll(end, 20, 1), pltpu.roll(end, 12, 1)),
            ),
        )

    for i in range(PARTS):
        landed(i)
        wrap = solve(i)
        for k, d in enumerate(others):
            finish(i, d, wrap)
            if k > 0:
                back_copy(i, others[k - 1], me).start()
        finish(i, me, wrap)
        back_copy(i, others[-1], me).start()
    back[me] = corr[me]

    for copy in normal:
        copy.wait_send()

    def in_sent(k, carry):
        p = lax.rem(me + k, ntm)
        in_copy(1, 0, p, 2 * p + 1).wait_send()
        in_copy(0, PARTS - 1, p, 2 * p).wait_send()
        return carry

    lax.fori_loop(1, ntm, in_sent, 0)

    def back_landed(k, carry):
        p = lax.rem(me + k, ntm)
        for i in range(PARTS):
            copy = back_copy(i, p, p)
            copy.wait_send()
            copy.wait_recv()
        return carry

    lax.fori_loop(1, ntm, back_landed, 0)

    for b in range(cols // 128):
        here = pl.ds(128 * b, 128)
        pieces = [(b * (128 // width) + p, i) for p in range(128 // width) for i in range(PARTS)]
        first_part = jnp.concatenate([back[p, i, 0:own] for p, i in pieces], axis=0).T
        rest = []
        for p, i in pieces:
            piece = back[p, i, own : own + half]
            rest += [piece, pltpu.roll(piece, 64, 1)]
        second_part = jnp.concatenate(rest, axis=0).T
        for f in range(3):
            out[0, f, :, here] = state[0, f, :, here] - first_part[32 * f : 32 * f + 32]
        out[1, 0, :, here] = state[1, 0, :, here] - first_part[96:128]
        for f in (1, 2):
            out[1, f, :, here] = state[1, f, :, here] - second_part[32 * f - 32 : 32 * f]


def solution(mesh):
    ntm, nsp = mesh.shape["tm"], mesh.shape["space"]

    def on_device(state, initial):
        cols = state.shape[3]
        width = cols // ntm
        vmem = pltpu.VMEM
        return pl.pallas_call(
            functools.partial(kernel, ntm, nsp),
            out_shape=jax.ShapeDtypeStruct(state.shape, f32),
            in_specs=[pl.BlockSpec(memory_space=pl.ANY)] * 3,
            out_specs=pl.BlockSpec(memory_space=vmem),
            scratch_shapes=[
                vmem(state.shape, f32),
                vmem((256, 256), jnp.bfloat16),
                vmem((2, 3, 8, cols), f32),
                vmem((3, 32, cols), f32),
                vmem((3, 8, cols), f32),
                vmem((128, cols), f32),
                vmem((2, ntm, width + 16, 128), f32),
                vmem((2 * ntm, width + 16, 128), f32),
                vmem((2 * ntm, width // PARTS + 8, 128), f32),
                vmem((ntm, PARTS, 3 * width // (2 * PARTS), 128), f32),
                vmem((ntm, PARTS, 3 * width // (2 * PARTS), 128), f32),
                pltpu.SemaphoreType.DMA((7,)),
                pltpu.SemaphoreType.DMA((7,)),
                pltpu.SemaphoreType.DMA((2, PARTS, ntm)),
                pltpu.SemaphoreType.DMA((2, PARTS, ntm)),
                pltpu.SemaphoreType.DMA((PARTS, ntm)),
                pltpu.SemaphoreType.DMA((PARTS, ntm)),
                pltpu.SemaphoreType.DMA((3,)),
                pltpu.SMEM((ntm,), f32),
            ],
            compiler_params=pltpu.CompilerParams(
                collective_id=0, has_side_effects=True, vmem_limit_bytes=60 << 20
            ),
        )(state, initial, stencil_table())

    return jax.shard_map(
        on_device,
        mesh=mesh,
        in_specs=(P("tm", None, "space", None), P(None, "space", None)),
        out_specs=P("tm", None, "space", None),
        check_vma=False,
    )
```

time: 55.1 us -> 51.6 us (0.936)
  Pallas kernels: 52.8 us -> 49.3 us
    pallas_call x1, Pallas kernels: 52.8 us -> 49.3 us  [on_device(): pl.pallas_call(functools.partial(kernel, ntm, nsp), out_shape=jax.ShapeDt...]
where the time goes in v3:
time: 51.6 us; the launch traced here: 51.4 us
  Pallas kernels  49.3 us (96%)
  local copies, waits for them, and re-layouts  2.09 us (4%)
    pallas_call x1, Pallas kernels, on_device(): pl.pallas_call(functools.partial(kernel, ntm, nsp), out_shape=jax.ShapeDt...  49.3 us
    unnamed x1, local copies, waits for them, and re-layouts  2.09 us

profile of v3, /device:TPU:1, one launch (start us, length us, event | category | flops | bytes accessed | tf_op | source)
XLA Modules:
  0.0 51.4 jit_solution(12806653382320894984)
XLA Ops:
  0.0 49.3 %shard_map.37 = f32[2,3,32,1024]{3,2,1,0:T(8,128)} custom-call(f32[2,3,32,1024]{3,2,1,0:T(8,128)} %state_hbm.1, f32[3,32,1024]{2,1,0:T(8,128)} %initial.1, bf16[256,256]{1,0:T(8,128)(2,1)} %constant.2.clone.stencil_hbm), custom_call_target="tpu_custom_call" | custom-call | tf_op jit(solution)/shard_map/pallas_call | solution.py:421
  49.3 2.1 %copy.5 = f32[2,3,32,1024]{3,2,1,0:T(8,128)} copy(f32[2,3,32,1024]{3,2,1,0:T(8,128)} %shard_map.37) | data formatting | bytes 1572864

commit v4 on v3

--- a/solution.py
+++ b/solution.py
@@ -40,7 +40,7 @@
         table[0, R + r, 2 * R + r] = -6.0
         table[1, R + r, r] = table[1, r, R + r] = -5.0
     one = np.concatenate(list(table), axis=1)
-    return jnp.asarray(np.concatenate([one, one], axis=0), jnp.bfloat16)
+    return jnp.asarray(0.25 * np.concatenate([one, one], axis=0), jnp.bfloat16)
 
 
 def far_first(shape):
@@ -294,15 +294,15 @@
             for q in range(CHUNK):
                 n = CHUNK * k + q
                 h = A * (rhs(n) + h)
-                y_buf[n] = (0.05 * weights[0]) * h
+                y_buf[n] = (0.2 * weights[0]) * h
             return h
 
         h = lax.fori_loop(0, steps // CHUNK, first, zero)
-        wrap = (0.05 * A * weights[0] * closing) * h
+        wrap = (0.2 * A * weights[0] * closing) * h
         for m in range(1, SWEEPS):
-            keep, gain = 1.0 - weights[m], 0.05 * weights[m]
+            keep, gain = 1.0 - weights[m], 0.2 * weights[m]
             if m == SWEEPS - 1:
-                keep, gain = 20.0 * keep, 20.0 * gain
+                keep, gain = 5.0 * keep, 5.0 * gain
 
             def sweep(k, carry, keep=keep, gain=gain):
                 h, wrap = carry
@@ -318,7 +318,7 @@
                 for q in range(CHUNK):
                     n = CHUNK * k + q
                     part = mixed[rows * q : rows * q + rows]
-                    here, cross, even = part[:, :128], part[:, 128:], 4.0 * ys[q]
+                    here, cross, even = part[:, :128], part[:, 128:], ys[q]
                     beside = pltpu.roll(even + cross, rows - 1, 0) + pltpu.roll(even - cross, 1, 0)
                     h = A * (((rhs(n) + here) + beside) + h)
                     y_buf[n] = keep * ys[q] + gain * h
@@ -385,30 +385,45 @@
 
     lax.fori_loop(1, ntm, in_sent, 0)
 
-    def back_landed(k, carry):
+    per = 128 // width
+    pairs = shape[1] * 2 // per
+    pair = lax.div(z * 2, per)
+    for dx in sorted(range(shape[0]), key=lambda d: -min(d, shape[0] - d)):
+        for dz in range(pairs - 1, -1, -1):
+            b = lax.rem(x + dx, shape[0]) * pairs + lax.rem(pair + dz, pairs)
+            for k in range(per):
+                p = b * per + k
+                if dx == 0 and dz == 0:
+
+                    @pl.when(p != me)
+                    def _():
+                        for i in range(PARTS):
+                            back_copy(i, p, p).wait_recv()
+
+                else:
+                    for i in range(PARTS):
+                        back_copy(i, p, p).wait_recv()
+            here = pl.ds(pl.multiple_of(128 * b, 128), 128)
+            pieces = [(b * per + k, i) for k in range(per) for i in range(PARTS)]
+            first_part = jnp.concatenate([back[p, i, 0:own] for p, i in pieces], axis=0).T
+            rest = []
+            for p, i in pieces:
+                piece = back[p, i, own : own + half]
+                rest += [piece, pltpu.roll(piece, 64, 1)]
+            second_part = jnp.concatenate(rest, axis=0).T
+            for f in range(3):
+                out[0, f, :, here] = state[0, f, :, here] - first_part[32 * f : 32 * f + 32]
+            out[1, 0, :, here] = state[1, 0, :, here] - first_part[96:128]
+            for f in (1, 2):
+                out[1, f, :, here] = state[1, f, :, here] - second_part[32 * f - 32 : 32 * f]
+
+    def back_sent(k, carry):
         p = lax.rem(me + k, ntm)
         for i in range(PARTS):
-            copy = back_copy(i, p, p)
-            copy.wait_send()
-            copy.wait_recv()
+            back_copy(i, p, me).wait_send()
         return carry
 
-    lax.fori_loop(1, ntm, back_landed, 0)
-
-    for b in range(cols // 128):
-        here = pl.ds(128 * b, 128)
-        pieces = [(b * (128 // width) + p, i) for p in range(128 // width) for i in range(PARTS)]
-        first_part = jnp.concatenate([back[p, i, 0:own] for p, i in pieces], axis=0).T
-        rest = []
-        for p, i in pieces:
-            piece = back[p, i, own : own + half]
-            rest += [piece, pltpu.roll(piece, 64, 1)]
-        second_part = jnp.concatenate(rest, axis=0).T
-        for f in range(3):
-            out[0, f, :, here] = state[0, f, :, here] - first_part[32 * f : 32 * f + 32]
-        out[1, 0, :, here] = state[1, 0, :, here] - first_part[96:128]
-        for f in (1, 2):
-            out[1, f, :, here] = state[1, f, :, here] - second_part[32 * f - 32 : 32 * f]
+    lax.fori_loop(1, ntm, back_sent, 0)
 
 
 def solution(mesh):
@@ -418,9 +433,9 @@
         cols = state.shape[3]
         width = cols // ntm
         vmem = pltpu.VMEM
-        return pl.pallas_call(
+        updated = pl.pallas_call(
             functools.partial(kernel, ntm, nsp),
-            out_shape=jax.ShapeDtypeStruct(state.shape, f32),
+            out_shape=vmem(state.shape, f32),
             in_specs=[pl.BlockSpec(memory_space=pl.ANY)] * 3,
             out_specs=pl.BlockSpec(memory_space=vmem),
             scratch_shapes=[
@@ -448,6 +463,7 @@
                 collective_id=0, has_side_effects=True, vmem_limit_bytes=60 << 20
             ),
         )(state, initial, stencil_table())
+        return updated
 
     return jax.shard_map(
         on_device,

time: 51.6 us -> 49.2 us (0.953)
  local copies, waits for them, and re-layouts: 2.09 us -> 0.88 us
  Pallas kernels: 49.3 us -> 48.2 us
    unnamed x1, local copies, waits for them, and re-layouts: 2.09 us -> 0.88 us
    pallas_call x1, Pallas kernels: 49.3 us -> 48.2 us  [on_device(): pl.pallas_call(functools.partial(kernel, ntm, nsp), out_shape=vmem(state....]
where the time goes in v4:
time: 49.2 us; the launch traced here: 49.1 us
  Pallas kernels  48.2 us (98%)
  local copies, waits for them, and re-layouts  0.88 us (2%)
    pallas_call x1, Pallas kernels, on_device(): pl.pallas_call(functools.partial(kernel, ntm, nsp), out_shape=vmem(state....  48.2 us

profile of v4, /device:TPU:1, one launch (start us, length us, event | category | flops | bytes accessed | tf_op | source)
XLA Modules:
  0.0 49.1 jit_solution(15575622832394104810)
XLA Ops:
  0.0 48.2 %shard_map.37 = f32[2,3,32,1024]{3,2,1,0:T(8,128)S(1)} custom-call(f32[2,3,32,1024]{3,2,1,0:T(8,128)} %state_hbm.1, f32[3,32,1024]{2,1,0:T(8,128)} %initial.1, bf16[256,256]{1,0:T(8,128)(2,1)} %constant.2.clone.stencil_hbm), custom_call_target="tpu_custom_call" | custom-call | tf_op jit(solution)/shard_map/pallas_call | solution.py:436
  48.2 0.9 %copy.5 = f32[2,3,32,1024]{3,2,1,0:T(8,128)} copy(f32[2,3,32,1024]{3,2,1,0:T(8,128)S(1)} %shard_map.37) | data formatting | bytes 1572864

commit v5 on v4

--- a/solution.py
+++ b/solution.py
@@ -123,29 +123,25 @@
     width = cols // ntm
     sub8 = lax.broadcasted_iota(jnp.int32, (8, 1), 0)
 
-    def clear(n, carry):
-        s_buf[n, 0:8, :] = jnp.zeros((8, 128), f32)
-        s_buf[n, 8 + width : 16 + width, :] = jnp.zeros((8, 128), f32)
-        return carry
-
-    lax.fori_loop(0, steps, clear, 0, unroll=8)
     barrier = pltpu.get_barrier_semaphore()
     around = [(me, up), (me, dn), (nxt, up), (nxt, dn), (prv, up), (prv, dn)]
     for other in around:
         pl.semaphore_signal(barrier, inc=1, device_id=other, device_id_type=MESH)
 
-    def greet(k, carry):
-        pl.semaphore_signal(
-            barrier, inc=1, device_id=(lax.rem(me + k, ntm), sp), device_id_type=MESH
-        )
-        return carry
-
-    lax.fori_loop(1, ntm, greet, 0)
+    for p in others:
+        pl.semaphore_signal(barrier, inc=1, device_id=(p, sp), device_id_type=MESH)
     loads = [
         pltpu.make_async_copy(state_hbm.at[t], state.at[t], load_sem.at[t]) for t in (1, 0)
     ] + [pltpu.make_async_copy(stencil_hbm, stencil, load_sem.at[2])]
     for copy in loads:
         copy.start()
+
+    def clear(n, carry):
+        s_buf[n, 0:5, :] = jnp.zeros((5, 128), f32)
+        s_buf[n, 11 + width : 16 + width, :] = jnp.zeros((5, 128), f32)
+        return carry
+
+    lax.fori_loop(0, steps, clear, 0, unroll=8)
     pl.semaphore_wait(barrier, ntm - 1 + len(around))
 
     def exchange(i, src, dst, device):
@@ -161,10 +157,10 @@
     low, high = pl.ds(0, 4), pl.ds(4, 4)
     rows_hi = pl.ds(28, 4)
 
-    def edges(t):
+    def edges():
         return [
-            exchange(2 * t, state_hbm.at[t, :, low], halo.at[t, :, low], (me, dn)),
-            exchange(2 * t + 1, state_hbm.at[t, :, rows_hi], halo.at[t, :, high], (me, up)),
+            exchange(0, state_hbm.at[:, :, low], halo.at[:, :, low], (me, dn)),
+            exchange(1, state_hbm.at[:, :, rows_hi], halo.at[:, :, high], (me, up)),
         ]
 
     def handed(last):
@@ -174,13 +170,13 @@
             exchange(6, last.at[:, rows_hi], prev_halo.at[:, high], (nxt, up)),
         ]
 
-    normal = edges(0) + edges(1) + handed(state_hbm.at[1])
-    for copy in normal[:4]:
+    normal = edges() + handed(state_hbm.at[1])
+    for copy in normal[:2]:
         copy.start()
 
     @pl.when(me != ntm - 1)
     def _():
-        for copy in normal[4:]:
+        for copy in normal[2:]:
             copy.start()
 
     @pl.when(me == ntm - 1)
@@ -230,15 +226,11 @@
         for b in range(cols // 128):
             block = res[:, 128 * b : 128 * b + 128].T
             for i in range(128 // width):
-                send[t, b * (128 // width) + i, 8 : 8 + width, :] = block[width * i : width * i + width]
-
-        def margin(p, carry):
-            right, left = lax.rem(p + 1, ntm), lax.rem(p + ntm - 1, ntm)
-            send[t, p, 4:8, :] = send[t, left, 4 + width : 8 + width, :]
-            send[t, p, 8 + width : 12 + width, :] = send[t, right, 8:12, :]
-            return carry
-
-        lax.fori_loop(0, ntm, margin, 0)
+                p = b * (128 // width) + i
+                mine = block[width * i : width * i + width]
+                send[t, p, 8 : 8 + width, :] = mine
+                send[t, (p + 1) % ntm, 4:8, :] = mine[width - 4 :]
+                send[t, (p - 1) % ntm, 8 + width : 12 + width, :] = mine[:4]
 
     def go(t, i):
         for p in others:
@@ -250,11 +242,11 @@
         gain = gain * (A * A)
     for copy in loads:
         copy.wait()
-    for copy in normal[:4]:
+    for copy in normal[:2]:
         copy.wait_recv()
     step_out(1)
     go(1, 0)
-    for copy in normal[4:]:
+    for copy in normal[2:]:
         copy.wait_recv()
     step_out(0)
     go(0, 0)
@@ -263,7 +255,7 @@
             in_copy(0, i - 1, p, 2 * me).wait_send()
             in_copy(0, i, p, 2 * me).start()
     for t in range(2):
-        s_buf[2 * me + t] = send[t, me]
+        s_buf[2 * me + t, 5 : 11 + width, :] = send[t, me, 5 : 11 + width, :]
 
     def landed(i):
         def one(k, carry):
@@ -301,10 +293,11 @@
         wrap = (0.2 * A * weights[0] * closing) * h
         for m in range(1, SWEEPS):
             keep, gain = 1.0 - weights[m], 0.2 * weights[m]
+            kept = rows
             if m == SWEEPS - 1:
-                keep, gain = 5.0 * keep, 5.0 * gain
-
-            def sweep(k, carry, keep=keep, gain=gain):
+                keep, gain, kept = 5.0 * keep, 5.0 * gain, own
+
+            def sweep(k, carry, keep=keep, gain=gain, kept=kept):
                 h, wrap = carry
                 ys = []
                 for q in range(CHUNK):
@@ -320,13 +313,14 @@
                     part = mixed[rows * q : rows * q + rows]
                     here, cross, even = part[:, :128], part[:, 128:], ys[q]
                     beside = pltpu.roll(even + cross, rows - 1, 0) + pltpu.roll(even - cross, 1, 0)
-                    h = A * (((rhs(n) + here) + beside) + h)
-                    y_buf[n] = keep * ys[q] + gain * h
+                    s = rhs(n) if kept == rows else s_buf[n, start : start + own, :]
+                    h = A * (((s + here[:kept]) + beside[:kept]) + h)
+                    y_buf[n, 0:kept, :] = keep * ys[q][:kept] + gain * h
                 return h, wrap
 
-            h, _ = lax.fori_loop(0, steps // CHUNK, sweep, (zero, wrap))
+            h, _ = lax.fori_loop(0, steps // CHUNK, sweep, (zero[:kept], wrap))
             wrap = (gain * A * closing) * h
-        return wrap[0:own, :]
+        return wrap
 
     def back_copy(i, d, slot):
         return pltpu.make_async_remote_copy(

time: 49.2 us -> 48.9 us (level)
  Pallas kernels: 48.2 us -> 47.5 us
    pallas_call x1, Pallas kernels: 48.2 us -> 47.5 us  [on_device(): pl.pallas_call(functools.partial(kernel, ntm, nsp), out_shape=vmem(state....]
where the time goes in v5:
time: 48.9 us; the launch traced here: 48.4 us
  Pallas kernels  47.5 us (97%)
  local copies, waits for them, and re-layouts  0.88 us (2%)
    pallas_call x1, Pallas kernels, on_device(): pl.pallas_call(functools.partial(kernel, ntm, nsp), out_shape=vmem(state....  47.5 us

profile of v5, /device:TPU:1, one launch (start us, length us, event | category | flops | bytes accessed | tf_op | source)
XLA Modules:
  0.0 48.4 jit_solution(1508375322403966684)
XLA Ops:
  0.0 47.5 %shard_map.37 = f32[2,3,32,1024]{3,2,1,0:T(8,128)S(1)} custom-call(f32[2,3,32,1024]{3,2,1,0:T(8,128)} %state_hbm.1, f32[3,32,1024]{2,1,0:T(8,128)} %initial.1, bf16[256,256]{1,0:T(8,128)(2,1)} %constant.2.clone.stencil_hbm), custom_call_target="tpu_custom_call" | custom-call | tf_op jit(solution)/shard_map/pallas_call | solution.py:430
  47.5 0.9 %copy.5 = f32[2,3,32,1024]{3,2,1,0:T(8,128)} copy(f32[2,3,32,1024]{3,2,1,0:T(8,128)S(1)} %shard_map.37) | data formatting | bytes 1572864

commit v6 on v5

--- a/solution.py
+++ b/solution.py
@@ -12,7 +12,7 @@
 SWEEPS = 4
 ALPHA = 0.1
 A = 1.0 / 1.8
-CHUNK = 32
+CHUNK = 64
 PARTS = 1
 R = 40
 MESH = pl.DeviceIdType.MESH

time: 48.9 us -> 48.8 us (level)
  no operation moved by 1% of the time
where the time goes in v6:
time: 48.8 us; the launch traced here: 48.2 us
  Pallas kernels  47.3 us (97%)
  local copies, waits for them, and re-layouts  0.88 us (2%)
    pallas_call x1, Pallas kernels, on_device(): pl.pallas_call(functools.partial(kernel, ntm, nsp), out_shape=vmem(state....  47.3 us

profile of v6, /device:TPU:1, one launch (start us, length us, event | category | flops | bytes accessed | tf_op | source)
XLA Modules:
  0.0 48.2 jit_solution(1764035767256850453)
XLA Ops:
  0.0 47.3 %shard_map.37 = f32[2,3,32,1024]{3,2,1,0:T(8,128)S(1)} custom-call(f32[2,3,32,1024]{3,2,1,0:T(8,128)} %state_hbm.1, f32[3,32,1024]{2,1,0:T(8,128)} %initial.1, bf16[256,256]{1,0:T(8,128)(2,1)} %constant.2.clone.stencil_hbm), custom_call_target="tpu_custom_call" | custom-call | tf_op jit(solution)/shard_map/pallas_call | solution.py:430
  47.3 0.9 %copy.5 = f32[2,3,32,1024]{3,2,1,0:T(8,128)} copy(f32[2,3,32,1024]{3,2,1,0:T(8,128)S(1)} %shard_map.37) | data formatting | bytes 1572864
